TPU v7x, 256 devices: a whole 4x4x8 slice. The times are simulated.
256 devices in a mesh: ctx: 128 (over z, y_lo, x, core), head: 2 (over y_hi).
Axes of the slice: x: 4, y: 4 (y_hi: 2, y_lo: 2; y = y_hi * 2 + y_lo), z: 8, core: 2. Of those that a mesh axis runs over, the one named last changes fastest.
Arguments:
- queries: bfloat16 [65536, 4096], P('ctx', 'head'), may hold values from -10 to 10
- key_states: bfloat16 [65536, 1024], P('ctx', 'head'), may hold values from -10 to 10
- value_rows_stored: bfloat16 [65536, 1024], P('ctx', 'head'), may hold values from -6 to 6
- span_order: int32 [128, 4], replicated, may hold values from 0 to 3, each once within a row
- doc_lengths: int32 [128], replicated, may hold values from 1 to 1792, 65536 in all
- w_out: bfloat16 [4096, 4096], P('ctx', 'head'), may hold values from -0.09375 to 0.09375
Outputs:
- projected: bfloat16 [65536, 4096], P('ctx', 'head')
Inputs may be any that keep to these rules, and one draw needn't show every extreme that they name: `span_order`: each row is a permutation of 0 to 3, so each shard holds the 4 spans of its own 512 consecutive positions in some order. `doc_lengths`: the lengths sum to 65536; the longest is exactly 1792.
All inputs are finite; a program needn't handle non-finite values.
Results may differ from a plain program's by a relative error of at most 0.0055.
Values may be sent and summed in bfloat16 or wider, within the bound.
A program may use at most 128 MiB of HBM per device.

v0:
```python
import math

import jax
import jax.numpy as jnp
from jax import lax
from jax.experimental import pallas as pl
from jax.experimental.pallas import tpu as pltpu
from jax.sharding import PartitionSpec as P

MESH = pl.DeviceIdType.MESH
BF16 = jnp.bfloat16
F32 = jnp.float32
HD = 128
BLK = 128
ROWS = 512
NX, NY, NZ = 4, 2, 8
NG = 4
WIN = 15 * BLK
NA = 1280
NB = 2048 - NA
SCALE = math.log2(math.e) / math.sqrt(HD)
NEG = -1e30

AX, AY, AZ, AM = 0, 3, 4, 12
BZ, BY, BX, BM = 21, 28, 29, 32
N_W = 36


def kernel(so_ref, lens_ref, q_ref, k_ref, v_ref, w_ref, out_ref,
           kv, wa, wb, att, acca, accb, st_ref, kvs, kvr, ws, wr, ats, atr):
    c = lax.axis_index("ctx")
    h = lax.axis_index("head")
    core = lax.rem(c, 2)
    chip = lax.div(c, 2)
    x = lax.rem(chip, NX)
    yl = lax.rem(lax.div(chip, NX), NY)
    z = lax.div(chip, NX * NY)

    def dev(z_, y_, x_, core_, h_):
        return (((z_ * NY + y_) * NX + x_) * 2 + core_, h_)

    def along(by, core_):
        return (lax.rem(chip + by + 64, 64) * 2 + core_, h)

    def zz(by):
        return lax.rem(z + by + NZ, NZ)

    def xx(by):
        return lax.rem(x + by + NX, NX)

    mate = (chip * 2 + 1 - core, h)
    xp, xm = dev(z, yl, xx(1), core, h), dev(z, yl, xx(-1), core, h)
    zp, zm = dev(zz(1), yl, x, core, h), dev(zz(-1), yl, x, core, h)
    yo = dev(z, 1 - yl, x, core, h)
    ho = (c, 1 - h)

    barrier = pltpu.get_barrier_semaphore()

    def signal(to):
        pl.semaphore_signal(barrier, inc=1, device_id=to, device_id_type=MESH)

    for to in (mate, xp, xm, zp, zm, yo, ho, along(-1, core)):
        signal(to)

    @pl.when(core == 0)
    def _():
        signal(along(-2, 0))
        signal(along(-2, 1))

    order = [so_ref[c, j] for j in range(4)]

    def held(ref, span, cols):
        parts = [ref[j * BLK:(j + 1) * BLK, cols] for j in range(4)]
        part = parts[3]
        for j in (2, 1, 0):
            part = jnp.where(order[j] == span, parts[j], part)
        return part

    for b in range(4):
        for g in range(NG):
            at = pl.ds((14 + b) * BLK, BLK)
            kv[g, at, 0:HD] = held(k_ref, b, slice(g * HD, (g + 1) * HD))
            kv[g, at, HD:2 * HD] = held(v_ref, b, slice(g * HD, (g + 1) * HD))
    wa[z, yl, x, core] = w_ref[:, 0:NA]
    wb[z, yl, x, core] = w_ref[:, NA:2048]

    lens = lens_ref[...]
    high = lax.div(lens, 64)
    low = lens - high * 64
    upto = (lax.broadcasted_iota(jnp.int32, (128, 128), 0)
            <= lax.broadcasted_iota(jnp.int32, (128, 128), 1)).astype(F32).astype(BF16)

    def running(part):
        wide = jnp.broadcast_to(part.astype(F32), (16, 128)).astype(BF16)
        return jnp.dot(wide, upto, preferred_element_type=F32)[0:1, :]

    ends = running(high) * 64.0 + running(low)
    pos = (lax.broadcasted_iota(jnp.int32, (ROWS, 128), 0) + c * ROWS).astype(F32)
    begun = jnp.where(ends <= pos, ends, 0.0)
    first = jnp.max(begun, axis=1, keepdims=True)
    blk = lax.div(lax.broadcasted_iota(jnp.int32, (ROWS, 128), 0), BLK)
    origin = (blk * BLK + (c * ROWS - 14 * BLK)).astype(F32)
    st_ref[...] = jnp.broadcast_to(first, (ROWS, 128)) - origin

    acca[...] = jnp.zeros_like(acca)
    accb[...] = jnp.zeros_like(accb)

    pl.semaphore_wait(barrier, 9)

    def kv_at(g, tile, tiles):
        return kv.at[g, pl.ds(tile * BLK, tiles * BLK)]

    def kv_copy(g, src, dst, tiles, number, slot, to):
        return pltpu.make_async_remote_copy(
            src_ref=kv_at(g, src, tiles), dst_ref=kv_at(g, dst, tiles),
            send_sem=kvs.at[g, number], recv_sem=kvr.at[g, slot],
            device_id=to, device_id_type=MESH)

    def near0(g):
        return [kv_copy(g, 14, 6, 4, 0, 1, along(1, 0)),
                kv_copy(g, 14, 10, 4, 1, 0, mate),
                kv_copy(g, 16, 0, 2, 2, 3, along(2, 0))]

    def near1(g):
        return [kv_copy(g, 14, 6, 4, 0, 1, along(1, 1)),
                kv_copy(g, 14, 2, 4, 2, 2, along(2, 0))]

    def pass0(g):
        return [kv_copy(g, 6, 2, 4, 3, 2, mate), kv_copy(g, 4, 0, 2, 4, 3, mate)]

    def pass1(g):
        return [kv_copy(g, 6, 10, 4, 3, 0, mate)]

    def kv_wait(g, slot):
        tile, tiles = ((10, 4), (6, 4), (2, 4), (0, 2))[slot]
        kv_copy(g, tile, tile, tiles, 0, slot, mate).wait_recv()

    def kv_send(g):
        @pl.when(core == 0)
        def _():
            for copy in near0(g):
                copy.start()

        @pl.when(core == 1)
        def _():
            for copy in near1(g):
                copy.start()

    def kv_pass(g):
        @pl.when(core == 0)
        def _():
            one, two = pass0(g)
            kv_wait(g, 1)
            one.start()
            kv_wait(g, 2)
            two.start()

        @pl.when(core == 1)
        def _():
            kv_wait(g, 1)
            for copy in pass1(g):
                copy.start()

    def kv_rest(g):
        @pl.when(core == 0)
        def _():
            kv_wait(g, 0)
            kv_wait(g, 3)

        @pl.when(core == 1)
        def _():
            kv_wait(g, 0)
            kv_wait(g, 2)
            kv_wait(g, 3)

    def kv_drain(g):
        @pl.when(core == 0)
        def _():
            for copy in near0(g) + pass0(g):
                copy.wait_send()

        @pl.when(core == 1)
        def _():
            for copy in near1(g) + pass1(g):
                copy.wait_send()

    def put(part, number, to, src=None):
        return lambda: pltpu.make_async_remote_copy(
            src_ref=part if src is None else src, dst_ref=part,
            send_sem=ws.at[number], recv_sem=wr.at[number], device_id=to, device_id_type=MESH)

    def entry(part, number, to, got_part, src=None):
        return put(part, number, to, src), number, got_part

    def a_block(x_):
        return wa.at[z, yl, x_, core]

    def a_row(y_):
        return wa.at[z, y_, :, core]

    def a_group(z_, core_=None):
        return wa.at[z_, :, :, core if core_ is None else core_]

    def a_half(z_, y_, core_=None):
        return wa.at[z_, y_, :, core if core_ is None else core_]

    def b_block(z_):
        return wb.at[z_, yl, x, core]

    def b_line(y_):
        return wb.at[:, y_, x, core]

    def b_group(x_, core_=None):
        return wb.at[:, :, x_, core if core_ is None else core_]

    own_a, own_b = w_ref.at[:, pl.ds(0, NA)], w_ref.at[:, pl.ds(NA, NB)]
    ax = [entry(a_block(x), AX, xp, a_block(xx(-1)), own_a),
          entry(a_block(x), AX + 1, xm, a_block(xx(1)), own_a),
          entry(a_block(xx(1)), AX + 2, xm, a_block(xx(2)))]
    ay = entry(a_row(yl), AY, yo, a_row(1 - yl))
    az = []
    for s in range(3):
        az.append(entry(a_group(zz(-s)), AZ + 2 * s, zp, a_group(zz(-s - 1))))
        az.append(entry(a_group(zz(s)), AZ + 2 * s + 1, zm, a_group(zz(s + 1))))
    az.append(entry(a_half(zz(-3), 0), AZ + 6, zp, a_half(zz(-4), 0)))
    az.append(entry(a_half(zz(3), 1), AZ + 7, zm, a_half(zz(4), 1)))
    am = [entry(a_group(z), AM, mate, a_group(z, 1 - core))]
    for s in range(3):
        am.append(entry(a_group(zz(-s - 1)), AM + 1 + 2 * s, mate, a_group(zz(-s - 1), 1 - core)))
        am.append(entry(a_group(zz(s + 1)), AM + 2 + 2 * s, mate, a_group(zz(s + 1), 1 - core)))
    am.append(entry(a_half(zz(4), 0), AM + 7, mate, a_half(zz(4), 0, 1 - core)))
    am.append(entry(a_half(zz(4), 1), AM + 8, mate, a_half(zz(4), 1, 1 - core)))
    bz = []
    for s in range(3):
        up_src = own_b if s == 0 else None
        bz.append(entry(b_block(zz(-s)), BZ + 2 * s, zp, b_block(zz(-s - 1)), up_src))
        bz.append(entry(b_block(zz(s)), BZ + 2 * s + 1, zm, b_block(zz(s + 1)), up_src))
    bz.append(entry(b_block(zz(-3)), BZ + 6, zp, b_block(zz(-4))))
    by = entry(b_line(yl), BY, yo, b_line(1 - yl))
    bx = [entry(b_group(x), BX, xp, b_group(xx(-1))),
          entry(b_group(x), BX + 1, xm, b_group(xx(1))),
          entry(b_group(xx(1)), BX + 2, xm, b_group(xx(2)))]
    bm = [entry(b_group(xx(d)), BM + i, mate, b_group(xx(d), 1 - core))
          for i, d in enumerate((0, -1, 1, 2))]

    def go(*entries):
        for copy, _, _ in entries:
            copy().start()

    def got(*entries):
        for _, number, part in entries:
            put(part, number, mate)().wait_recv()

    def att_copy(head, g, b):
        part = att.at[4 * head + g, pl.ds(b * BLK, BLK)]
        return pltpu.make_async_remote_copy(
            src_ref=part, dst_ref=part, send_sem=ats.at[g, b], recv_sem=atr.at[g, b],
            device_id=ho, device_id_type=MESH)

    go(ax[0], ax[1], bz[0], bz[1])
    kv_send(0)
    got(ax[1])
    go(ax[2])
    got(bz[0], bz[1])
    go(bz[2], bz[3])
    kv_send(1)
    got(ax[0], ax[2])
    go(ay)
    got(bz[2], bz[3])
    go(bz[4], bz[5])
    kv_send(2)
    got(bz[4], bz[5])
    go(bz[6])
    kv_send(3)
    got(bz[6])
    go(by)
    kv_pass(0)

    def ev_az1():
        got(ay)
        go(az[0], az[1], am[0])

    def ev_bx1():
        got(by)
        go(bx[0], bx[1], bm[0])

    def ev_az(s):
        def run():
            got(az[2 * s - 2], az[2 * s - 1])
            go(az[2 * s], az[2 * s + 1], am[2 * s - 1], am[2 * s])
        return run

    def ev_bx2():
        got(bx[1])
        go(bx[2], bm[2])

    def ev_kv(g):
        return lambda: kv_pass(g)

    before = {0: [ev_az1], 3: [ev_kv(1)], 4: [ev_bx1], 6: [ev_az(1)], 7: [ev_kv(2)],
              10: [ev_bx2], 11: [ev_kv(3)], 12: [ev_az(2)]}

    lane = lax.broadcasted_iota(jnp.int32, (BLK, WIN), 1).astype(F32)
    row = lax.broadcasted_iota(jnp.int32, (BLK, BLK), 0)
    causal = lax.broadcasted_iota(jnp.int32, (BLK, BLK), 1) <= row

    def unit(i, carry):
        g, b = lax.div(i, 4), lax.rem(i, 4)
        for at, runs in before.items():
            @pl.when(i == at)
            def _(runs=runs):
                for run in runs:
                    run()

        @pl.when(b == 0)
        def _():
            kv_rest(g)

        @pl.when(i > 0)
        def _():
            att_copy(h, lax.div(i - 1, 4), lax.rem(i - 1, 4)).start()

        q4 = held(q_ref, b, pl.ds(pl.multiple_of(g * 4 * HD, 4 * HD), 4 * HD))
        q = jnp.concatenate([q4[:, j * HD:(j + 1) * HD] for j in range(4)], axis=0)
        window = pl.ds(pl.multiple_of(b * BLK, BLK), WIN)
        k = kv[g, window, 0:HD]
        v = kv[g, window, HD:2 * HD]
        s = lax.dot_general(q, k, (((1,), (1,)), ((), ())), preferred_element_type=F32)
        st = st_ref[pl.ds(pl.multiple_of(b * BLK, BLK), BLK), :]
        far = lane[:, :14 * BLK] >= jnp.concatenate([st] * 14, axis=1)
        last = (lane[:, 14 * BLK:] >= st) & causal
        far4 = jnp.concatenate([far] * 4, axis=0)
        last4 = jnp.concatenate([last] * 4, axis=0)
        s = jnp.concatenate([jnp.where(far4, s[:, :14 * BLK], NEG),
                             jnp.where(last4, s[:, 14 * BLK:], NEG)], axis=1)
        m = jnp.max(s, axis=1, keepdims=True)
        p = jnp.exp2((s - m) * SCALE).astype(BF16)
        vo = jnp.concatenate([v, jnp.ones((WIN, HD), BF16)], axis=1)
        o = jnp.dot(p, vo, preferred_element_type=F32)
        a = (o[:, :HD] / o[:, HD:]).astype(BF16)
        a4 = jnp.concatenate([a[j * BLK:(j + 1) * BLK] for j in range(4)], axis=1)
        att[4 * h + g, pl.ds(pl.multiple_of(b * BLK, BLK), BLK), :] = a4
        return carry

    lax.fori_loop(0, 16, unit, 0)
    att_copy(h, 3, 3).start()

    got(az[4], az[5])
    go(az[6], az[7], am[5], am[6])
    got(bx[0])
    go(bm[1])
    got(bx[2])
    go(bm[3])
    got(az[6], az[7])
    go(am[7], am[8])
    got(*am)
    got(*bm)

    def project(j, carry):
        at = lax.rem(4 * h + j, 8)

        @pl.when(j >= 4)
        def _():
            for b in range(4):
                att_copy(1 - h, j - 4, b).wait_recv()

        a = att[at]
        acca[...] += jnp.dot(a, wa[at].reshape(ROWS, NA), preferred_element_type=F32)
        accb[...] += jnp.dot(a, wb[at].reshape(ROWS, NB), preferred_element_type=F32)
        return carry

    lax.fori_loop(0, 8, project, 0)
    def placed(ref, j):
        part = ref[3 * BLK:4 * BLK, :]
        for b in (2, 1, 0):
            part = jnp.where(order[j] == b, ref[b * BLK:(b + 1) * BLK, :], part)
        return part.astype(BF16)

    for j in range(4):
        out_ref[j * BLK:(j + 1) * BLK, 0:NA] = placed(acca, j)
        out_ref[j * BLK:(j + 1) * BLK, NA:2048] = placed(accb, j)

    for g in range(NG):
        kv_drain(g)
        for b in range(4):
            att_copy(h, g, b).wait_send()
    for copy, _, _ in ax + [ay] + az + am + bz + [by] + bx + bm:
        copy().wait_send()


def per_device(queries, key_states, value_rows_stored, span_order, doc_lengths, w_out):
    vmem = pl.BlockSpec(memory_space=pltpu.VMEM)
    return pl.pallas_call(
        kernel,
        out_shape=jax.ShapeDtypeStruct((ROWS, 2048), BF16),
        in_specs=[pl.BlockSpec(memory_space=pltpu.SMEM), vmem, vmem, vmem, vmem, vmem],
        out_specs=vmem,
        scratch_shapes=[
            pltpu.VMEM((NG, 18 * BLK, 2 * HD), BF16),
            pltpu.VMEM((NZ, NY, NX, 2, 32, NA), BF16),
            pltpu.VMEM((NZ, NY, NX, 2, 32, NB), BF16),
            pltpu.VMEM((8, ROWS, 4 * HD), BF16),
            pltpu.VMEM((ROWS, NA), F32),
            pltpu.VMEM((ROWS, NB), F32),
            pltpu.VMEM((ROWS, 128), F32),
            pltpu.SemaphoreType.DMA((NG, 5)),
            pltpu.SemaphoreType.DMA((NG, 4)),
            pltpu.SemaphoreType.DMA((N_W,)),
            pltpu.SemaphoreType.DMA((N_W,)),
            pltpu.SemaphoreType.DMA((NG, 4)),
            pltpu.SemaphoreType.DMA((NG, 4)),
        ],
        compiler_params=pltpu.CompilerParams(
            collective_id=0, has_side_effects=True, vmem_limit_bytes=63 * 1024 * 1024),
        name="attend_project",
    )(span_order, doc_lengths.reshape(1, 128), queries, key_states, value_rows_stored, w_out)


def solution(mesh):
    placed = (P("ctx", "head"), P("ctx", "head"), P("ctx", "head"), P(), P(), P("ctx", "head"))
    return jax.shard_map(
        per_device, mesh=mesh, in_specs=placed, out_specs=P("ctx", "head"), check_vma=False
    )
```

profile of v0, /device:TPU:1, one launch (start us, length us, event | category | flops | bytes accessed | tf_op | source)
XLA Modules:
  0.0 140.8 jit_solution(1095306609534881636)
XLA Ops:
  0.0 1.4 %copy.7.so_ref = s32[128,4]{1,0:T(8,128)} copy(s32[128,4]{0,1:T(4,128)} %param.9) | data formatting | bytes 4096 | tf_op args[3]
  1.4 136.2 %attend_project.1 = bf16[512,2048]{1,0:T(8,128)(2,1)} custom-call(s32[128,4]{1,0:T(8,128)} %copy.7.so_ref, s32[1,128]{1,0:T(1,128)} %bitcast.1, bf16[512,2048]{1,0:T(8,128)(2,1)} %q_ref.1, bf16[512,512]{1,0:T(8,128)(2,1)} %k_ref.1, bf16[512,512]{1,0:T(8,128)(2,1)} %v_ref.1, bf16[32,2048]{1,0:T(8,128)(2,1)} %w_ref.1), custom_call_target="tpu_custom_call" | custom-call | tf_op jit(solution)/shard_map/attend_project/pallas_call | solution.py:393
  137.6 3.2 %copy.9 = bf16[512,2048]{1,0:T(8,128)(2,1)} copy(bf16[512,2048]{1,0:T(8,128)(2,1)} %attend_project.1) | data formatting | bytes 4194304
where the time goes:
time: 141 us
  Pallas kernels  136 us (96%)
  local copies, waits for them, and re-layouts  4.57 us (3%)
    pallas_call x1, Pallas kernels, per_device(): pl.pallas_call(kernel, out_shape=jax.ShapeDtypeStruct((ROWS, 2048), BF16)...  136 us
    unnamed x2, local copies, waits for them, and re-layouts  4.57 us

commit v1 on v0

v1 whole, which is shorter than its diff:
```python
import math

import jax
import jax.numpy as jnp
from jax import lax
from jax.experimental import pallas as pl
from jax.experimental.pallas import tpu as pltpu
from jax.sharding import PartitionSpec as P

MESH = pl.DeviceIdType.MESH
BF16 = jnp.bfloat16
F32 = jnp.float32
HD = 128
BLK = 128
ROWS = 512
NX, NY, NZ = 4, 2, 8
NG = 4
WIN = 15 * BLK
NA = 1024
NB = 2048 - NA
SCALE = math.log2(math.e) / math.sqrt(HD)
NEG = -1e30

AX, AY, AZ, AM = 0, 3, 4, 32
BZ, BY, BX, BM = 40, 47, 48, 72
N_W = 76
VIA = (2, 3)


def kernel(so_ref, lens_ref, q_hbm, k_ref, v_ref, w_ref, out_ref,
           q_ref, kv, transit, wa, wb, att, acca, accb, st_ref, kvs, kvr, ts, tr, ws, wr, ats, atr, q_sem):
    q_copy = pltpu.make_async_copy(q_hbm, q_ref, q_sem)
    q_copy.start()
    c = lax.axis_index("ctx")
    h = lax.axis_index("head")
    core = lax.rem(c, 2)
    chip = lax.div(c, 2)
    x = lax.rem(chip, NX)
    yl = lax.rem(lax.div(chip, NX), NY)
    z = lax.div(chip, NX * NY)

    def dev(z_, y_, x_, core_, h_):
        return (((z_ * NY + y_) * NX + x_) * 2 + core_, h_)

    def along(by, core_):
        return (lax.rem(chip + by + 64, 64) * 2 + core_, h)

    def zz(by):
        return lax.rem(z + by + NZ, NZ)

    def xx(by):
        return lax.rem(x + by + NX, NX)

    mate = (chip * 2 + 1 - core, h)
    xp, xm = dev(z, yl, xx(1), core, h), dev(z, yl, xx(-1), core, h)
    zp, zm = dev(zz(1), yl, x, core, h), dev(zz(-1), yl, x, core, h)
    yo = dev(z, 1 - yl, x, core, h)
    ho = (c, 1 - h)

    barrier = pltpu.get_barrier_semaphore()

    def signal(to):
        pl.semaphore_signal(barrier, inc=1, device_id=to, device_id_type=MESH)

    for to in (mate, xp, xm, zp, zm, yo, ho, along(-1, core)):
        signal(to)

    @pl.when(core == 0)
    def _():
        signal(along(-1, 1))

    @pl.when(x == 0)
    def _():
        signal(along(-4, core))

    order = [so_ref[j, c] for j in range(4)]

    def held(ref, span, cols):
        parts = [ref[j * BLK:(j + 1) * BLK, cols] for j in range(4)]
        part = parts[3]
        for j in (2, 1, 0):
            part = jnp.where(order[j] == span, parts[j], part)
        return part

    for b in range(4):
        for g in range(NG):
            at = pl.ds((14 + b) * BLK, BLK)
            kv[g, at, 0:HD] = held(k_ref, b, slice(g * HD, (g + 1) * HD))
            kv[g, at, HD:2 * HD] = held(v_ref, b, slice(g * HD, (g + 1) * HD))
    wa[z, yl, x, core] = w_ref[:, 0:NA]
    wb[z, yl, x, core] = w_ref[:, NA:2048]

    lens = lens_ref[...]
    high = lax.div(lens, 64)
    low = lens - high * 64
    upto = (lax.broadcasted_iota(jnp.int32, (128, 128), 0)
            <= lax.broadcasted_iota(jnp.int32, (128, 128), 1)).astype(F32).astype(BF16)

    def running(part):
        wide = jnp.broadcast_to(part.astype(F32), (16, 128)).astype(BF16)
        return jnp.dot(wide, upto, preferred_element_type=F32)[0:1, :]

    ends = running(high) * 64.0 + running(low)
    pos = (lax.broadcasted_iota(jnp.int32, (ROWS, 128), 0) + c * ROWS).astype(F32)
    begun = jnp.where(ends <= pos, ends, 0.0)
    first = jnp.max(begun, axis=1, keepdims=True)
    blk = lax.div(lax.broadcasted_iota(jnp.int32, (ROWS, 128), 0), BLK)
    origin = (blk * BLK + (c * ROWS - 14 * BLK)).astype(F32)
    st_ref[...] = jnp.broadcast_to(first, (ROWS, 128)) - origin

    acca[...] = jnp.zeros_like(acca)
    accb[...] = jnp.zeros_like(accb)

    pl.semaphore_wait(barrier, 8 + core + jnp.where(x == 0, 1, 0))

    def kv_at(g, tile, tiles):
        return kv.at[g, pl.ds(tile * BLK, tiles * BLK)]

    def kv_copy(g, src, dst, tiles, number, slot, to):
        return pltpu.make_async_remote_copy(
            src_ref=kv_at(g, src, tiles), dst_ref=kv_at(g, dst, tiles),
            send_sem=kvs.at[g, number], recv_sem=kvr.at[g, slot],
            device_id=to, device_id_type=MESH)

    def own_near(g):
        return kv_copy(g, 14, 6, 4, 0, 1, along(1, core))

    def own_via(g):
        return pltpu.make_async_remote_copy(
            src_ref=kv_at(g, 14, 4), dst_ref=transit.at[VIA.index(g)],
            send_sem=kvs.at[g, 0], recv_sem=tr.at[VIA.index(g)], device_id=xp, device_id_type=MESH)

    def own_on(g):
        return pltpu.make_async_remote_copy(
            src_ref=transit.at[VIA.index(g)], dst_ref=kv_at(g, 6, 4),
            send_sem=ts.at[VIA.index(g)], recv_sem=kvr.at[g, 1], device_id=along(4, core),
            device_id_type=MESH)

    def own_mate(g):
        return kv_copy(g, 14, 10, 4, 1, 0, mate)

    def pass0(g):
        return [kv_copy(g, 8, 0, 2, 2, 3, along(1, 0)), kv_copy(g, 6, 2, 4, 3, 2, mate)]

    def pass1(g):
        return [kv_copy(g, 6, 2, 4, 2, 2, along(1, 0)), kv_copy(g, 6, 10, 4, 3, 0, mate)]

    def late0(g):
        return kv_copy(g, 4, 0, 2, 4, 3, mate)

    def kv_wait(g, slot):
        tile, tiles = ((10, 4), (6, 4), (2, 4), (0, 2))[slot]
        kv_copy(g, tile, tile, tiles, 0, slot, mate).wait_recv()

    def kv_send(g):
        if g in VIA:
            @pl.when(x < 3)
            def _():
                own_near(g).start()
        else:
            own_near(g).start()

        @pl.when(core == 0)
        def _():
            own_mate(g).start()

    def kv_via(g):
        @pl.when(x == 3)
        def _():
            own_via(g).start()

    def kv_on(g):
        @pl.when(x == 0)
        def _():
            own_via(g).wait_recv()
            own_on(g).start()

    def kv_pass(g):
        kv_wait(g, 1)

        @pl.when(core == 0)
        def _():
            for copy in pass0(g):
                copy.start()

        @pl.when(core == 1)
        def _():
            for copy in pass1(g):
                copy.start()

    def kv_late(g):
        kv_wait(g, 2)

        @pl.when(core == 0)
        def _():
            late0(g).start()

    def kv_rest(g):
        kv_wait(g, 0)
        kv_wait(g, 3)

    def kv_drain(g):
        own_near(g).wait_send()
        if g in VIA:
            @pl.when(x == 0)
            def _():
                own_on(g).wait_send()

        @pl.when(core == 0)
        def _():
            for copy in [own_mate(g)] + pass0(g) + [late0(g)]:
                copy.wait_send()

        @pl.when(core == 1)
        def _():
            for copy in pass1(g):
                copy.wait_send()

    def put(part, number, to, src=None):
        return lambda: pltpu.make_async_remote_copy(
            src_ref=part if src is None else src, dst_ref=part,
            send_sem=ws.at[number], recv_sem=wr.at[number], device_id=to, device_id_type=MESH)

    def entry(part, number, to, got_part, src=None):
        return put(part, number, to, src), number, got_part

    def a_block(y_):
        return wa.at[z, y_, x, core]

    def a_pair(x_):
        return wa.at[z, :, x_, core]

    def a_group(z_, core_=None):
        return wa.at[z_, :, :, core if core_ is None else core_]

    def b_block(y_):
        return wb.at[z, y_, x, core]

    def b_pair(z_):
        return wb.at[z_, :, x, core]

    def b_group(x_, core_=None):
        return wb.at[:, :, x_, core if core_ is None else core_]

    own_a, own_b = w_ref.at[:, pl.ds(0, NA)], w_ref.at[:, pl.ds(NA, NB)]
    ay = entry(a_block(yl), AY, yo, a_block(1 - yl), own_a)
    by = entry(b_block(yl), BY, yo, b_block(1 - yl), own_b)
    ax = [entry(a_pair(x), AX, xp, a_pair(xx(-1))),
          entry(a_pair(x), AX + 1, xm, a_pair(xx(1))),
          entry(a_pair(xx(1)), AX + 2, xm, a_pair(xx(2)))]
    xq = (x, xx(-1), xx(1), xx(2))

    def az(qs, s):
        def part(d, q):
            return wa.at[zz(d), :, xq[q], core]
        if s == 3:
            return [entry(part(3, q), AZ + 7 * q + 6, zm, part(4, q)) for q in qs]
        return ([entry(part(-s, q), AZ + 7 * q + 2 * s, zp, part(-s - 1, q)) for q in qs]
                + [entry(part(s, q), AZ + 7 * q + 2 * s + 1, zm, part(s + 1, q)) for q in qs])

    def bz(s):
        if s == 3:
            return [entry(b_pair(zz(3)), BZ + 6, zm, b_pair(zz(4)))]
        return [entry(b_pair(zz(-s)), BZ + 2 * s, zp, b_pair(zz(-s - 1))),
                entry(b_pair(zz(s)), BZ + 2 * s + 1, zm, b_pair(zz(s + 1)))]

    near = (0, -1, 1, -2, 2, -3, 3, 4)
    am = [entry(a_group(zz(d)), AM + i, mate, a_group(zz(d), 1 - core)) for i, d in enumerate(near)]

    def bx(js, way):
        def part(j, d):
            return wb.at[zz(near[j]), :, xx(d), core]
        if way == 0:
            return [entry(part(j, 0), BX + 3 * j, xp, part(j, -1)) for j in js]
        if way == 1:
            return [entry(part(j, 0), BX + 3 * j + 1, xm, part(j, 1)) for j in js]
        return [entry(part(j, 1), BX + 3 * j + 2, xm, part(j, 2)) for j in js]

    bm = [entry(b_group(xx(d)), BM + i, mate, b_group(xx(d), 1 - core))
          for i, d in enumerate((0, -1, 1, 2))]

    def go(*entries):
        for copy, _, _ in entries:
            copy().start()

    def got(*entries):
        for _, number, part in entries:
            put(part, number, mate)().wait_recv()

    def att_copy(head, g, b):
        part = att.at[4 * head + g, pl.ds(b * BLK, BLK)]
        return pltpu.make_async_remote_copy(
            src_ref=part, dst_ref=part, send_sem=ats.at[g, b], recv_sem=atr.at[g, b],
            device_id=ho, device_id_type=MESH)

    go(ay, by)
    kv_send(0)
    kv_send(1)
    got(ay, by)
    go(ax[1], *bz(0), *az((0,), 0), *bx((0,), 1))
    kv_pass(0)
    go(ax[0])
    kv_send(2)
    kv_via(2)
    got(ax[1])
    go(ax[2], *az((2,), 0))
    got(*bz(0))
    go(*bz(1), *bx((1, 2), 1))
    kv_pass(1)
    kv_send(3)
    kv_via(3)
    got(*bz(1))
    go(*bz(2), *bx((3, 4), 1))
    got(ax[2])
    go(*az((3,), 0))
    q_copy.wait()
    kv_late(0)

    def at1():
        got(*bz(2))
        go(*bz(3), *bx((5, 6), 1))
        got(*az((0,), 0))
        go(*az((0,), 1))
        got(ax[0])
        go(*az((1,), 0), am[0])

    def at2():
        kv_on(2)
        got(*bz(3))
        go(*bx((7,), 1), bm[0])

    def at3():
        kv_late(1)
        got(*az((2, 3), 0))
        go(*az((2, 3), 1))

    def at4():
        kv_pass(2)
        got(*az((1,), 0))
        go(*az((1,), 1), am[1], am[2])

    def at5():
        kv_on(3)
        got(*bx((0, 1, 2, 3), 1))
        go(*bx((0, 1, 2, 3), 2))

    def at6():
        got(*az((0, 2), 1))
        go(*az((0, 2), 2))

    def at7():
        kv_late(2)
        got(*az((3, 1), 1))
        go(*az((3, 1), 2), am[3], am[4])

    def at8():
        kv_pass(3)
        got(*bx((4, 5, 6, 7), 1))
        go(*bx((4, 5, 6, 7), 2), bm[2])
        go(*bx((0, 1, 2, 3), 0))

    def at9():
        got(*az((0, 2), 2))
        go(*az((0, 2), 3))
        go(*bx((4, 5, 6, 7), 0))

    def at11():
        kv_late(3)
        got(*az((3, 1), 2))
        go(*az((3, 1), 3), am[5], am[6])

    before = {1: at1, 2: at2, 3: at3, 4: at4, 5: at5, 6: at6, 7: at7, 8: at8, 9: at9, 11: at11}

    lane = lax.broadcasted_iota(jnp.int32, (BLK, WIN), 1).astype(F32)
    row = lax.broadcasted_iota(jnp.int32, (BLK, BLK), 0)
    causal = lax.broadcasted_iota(jnp.int32, (BLK, BLK), 1) <= row

    def unit(i, carry):
        g, b = lax.div(i, 4), lax.rem(i, 4)
        for at, run in before.items():
            pl.when(i == at)(run)

        @pl.when(b == 0)
        def _():
            kv_rest(g)

        @pl.when(i > 0)
        def _():
            att_copy(h, lax.div(i - 1, 4), lax.rem(i - 1, 4)).start()

        q4 = held(q_ref, b, pl.ds(pl.multiple_of(g * 4 * HD, 4 * HD), 4 * HD))
        q = jnp.concatenate([q4[:, j * HD:(j + 1) * HD] for j in range(4)], axis=0)
        window = pl.ds(pl.multiple_of(b * BLK, BLK), WIN)
        k = kv[g, window, 0:HD]
        v = kv[g, window, HD:2 * HD]
        s = lax.dot_general(q, k, (((1,), (1,)), ((), ())), preferred_element_type=F32)
        st = st_ref[pl.ds(pl.multiple_of(b * BLK, BLK), BLK), :]
        far = lane[:, :14 * BLK] >= jnp.concatenate([st] * 14, axis=1)
        last = (lane[:, 14 * BLK:] >= st) & causal
        far4 = jnp.concatenate([far] * 4, axis=0)
        last4 = jnp.concatenate([last] * 4, axis=0)
        s = jnp.concatenate([jnp.where(far4, s[:, :14 * BLK], NEG),
                             jnp.where(last4, s[:, 14 * BLK:], NEG)], axis=1)
        m = jnp.max(s, axis=1, keepdims=True)
        p = jnp.exp2((s - m) * SCALE).astype(BF16)
        vo = jnp.concatenate([v, jnp.ones((WIN, HD), BF16)], axis=1)
        o = jnp.dot(p, vo, preferred_element_type=F32)
        a = (o[:, :HD] / o[:, HD:]).astype(BF16)
        a4 = jnp.concatenate([a[j * BLK:(j + 1) * BLK] for j in range(4)], axis=1)
        att[4 * h + g, pl.ds(pl.multiple_of(b * BLK, BLK), BLK), :] = a4
        return carry

    lax.fori_loop(0, 16, unit, 0)
    att_copy(h, 3, 3).start()

    def project_a(j, carry):
        d = lax.rem(lax.div(j + 1, 2) * (2 * lax.rem(j, 2) - 1) + 8, 8)
        at = lax.rem(z + 8 - d, 8)

        @pl.when(j == 7)
        def _():
            got(*az((0, 1, 2, 3), 3))
            go(am[7])

        for i in range(8):
            @pl.when(j == i)
            def _(i=i):
                got(am[i])

        @pl.when(lax.div(at, 4) == 1 - h)
        def _():
            for b in range(4):
                att_copy(1 - h, lax.rem(at, 4), b).wait_recv()

        acca[...] += jnp.dot(att[at], wa[at].reshape(ROWS, NA), preferred_element_type=F32)
        return carry

    lax.fori_loop(0, 8, project_a, 0)
    got(*bx(range(8), 2))
    go(bm[3])
    got(*bx(range(8), 0))
    go(bm[1])
    got(*bm)

    def project_b(at, carry):
        accb[...] += jnp.dot(att[at], wb[at].reshape(ROWS, NB), preferred_element_type=F32)
        return carry

    lax.fori_loop(0, 8, project_b, 0)

    def placed(ref, j):
        part = ref[3 * BLK:4 * BLK, :]
        for b in (2, 1, 0):
            part = jnp.where(order[j] == b, ref[b * BLK:(b + 1) * BLK, :], part)
        return part.astype(BF16)

    for j in range(4):
        out_ref[j * BLK:(j + 1) * BLK, 0:NA] = placed(acca, j)
        out_ref[j * BLK:(j + 1) * BLK, NA:2048] = placed(accb, j)

    for g in range(NG):
        kv_drain(g)
        for b in range(4):
            att_copy(h, g, b).wait_send()
    for copy, _, _ in ax + [ay, by] + am + bm:
        copy().wait_send()
    for s in range(4):
        for copy, _, _ in az((0, 1, 2, 3), s) + bz(s):
            copy().wait_send()
    for way in range(3):
        for copy, _, _ in bx(range(8), way):
            copy().wait_send()


def per_device(queries, key_states, value_rows_stored, span_order, doc_lengths, w_out):
    vmem = pl.BlockSpec(memory_space=pltpu.VMEM)
    return pl.pallas_call(
        kernel,
        out_shape=jax.ShapeDtypeStruct((ROWS, 2048), BF16),
        in_specs=[pl.BlockSpec(memory_space=pltpu.SMEM), vmem, pl.BlockSpec(memory_space=pl.ANY), vmem, vmem, vmem],
        out_specs=vmem,
        scratch_shapes=[
            pltpu.VMEM((ROWS, 2048), BF16),
            pltpu.VMEM((NG, 18 * BLK, 2 * HD), BF16),
            pltpu.VMEM((len(VIA), 4 * BLK, 2 * HD), BF16),
            pltpu.VMEM((NZ, NY, NX, 2, 32, NA), BF16),
            pltpu.VMEM((NZ, NY, NX, 2, 32, NB), BF16),
            pltpu.VMEM((8, ROWS, 4 * HD), BF16),
            pltpu.VMEM((ROWS, NA), F32),
            pltpu.VMEM((ROWS, NB), F32),
            pltpu.VMEM((ROWS, 128), F32),
            pltpu.SemaphoreType.DMA((NG, 5)),
            pltpu.SemaphoreType.DMA((NG, 4)),
            pltpu.SemaphoreType.DMA((len(VIA),)),
            pltpu.SemaphoreType.DMA((len(VIA),)),
            pltpu.SemaphoreType.DMA((N_W,)),
            pltpu.SemaphoreType.DMA((N_W,)),
            pltpu.SemaphoreType.DMA((NG, 4)),
            pltpu.SemaphoreType.DMA((NG, 4)),
            pltpu.SemaphoreType.DMA,
        ],
        compiler_params=pltpu.CompilerParams(
            collective_id=0, has_side_effects=True, vmem_limit_bytes=63 * 1024 * 1024),
        name="attend_project",
    )(span_order.T, doc_lengths.reshape(1, 128), queries, key_states, value_rows_stored, w_out)


def solution(mesh):
    placed = (P("ctx", "head"), P("ctx", "head"), P("ctx", "head"), P(), P(), P("ctx", "head"))
    return jax.shard_map(
        per_device, mesh=mesh, in_specs=placed, out_specs=P("ctx", "head"), check_vma=False
    )
```

time: 141 us -> 137 us (0.972)
  the two profiles are of different devices: /device:TPU:1 before, /device:TPU:8 now
where the time goes in v1:
time: 137 us
  Pallas kernels  133 us (97%)
  local copies, waits for them, and re-layouts  3.16 us (2%)
    pallas_call x1, Pallas kernels, per_device(): pl.pallas_call(kernel, out_shape=jax.ShapeDtypeStruct((ROWS, 2048), BF16)...  133 us
    unnamed x1, local copies, waits for them, and re-layouts  3.16 us

profile of v1, /device:TPU:8, one launch (start us, length us, event | category | flops | bytes accessed | tf_op | source)
XLA Modules:
  0.0 136.5 jit_solution(4175293578813151978)
XLA Ops:
  0.0 133.4 %attend_project.1 = bf16[512,2048]{1,0:T(8,128)(2,1)} custom-call(s32[4,128]{1,0:T(4,128)} %bitcast.2, s32[1,128]{1,0:T(1,128)} %bitcast.3, bf16[512,2048]{1,0:T(8,128)(2,1)} %q_hbm.1, bf16[512,512]{1,0:T(8,128)(2,1)} %k_ref.1, bf16[512,512]{1,0:T(8,128)(2,1)} %v_ref.1, bf16[32,2048]{1,0:T(8,128)(2,1)} %w_ref.1), custom_call_target="tpu_custom_call" | custom-call | tf_op jit(solution)/shard_map/attend_project/pallas_call | solution.py:477
  133.4 3.2 %copy.8 = bf16[512,2048]{1,0:T(8,128)(2,1)} copy(bf16[512,2048]{1,0:T(8,128)(2,1)} %attend_project.1) | data formatting | bytes 4194304

commit v2 on v1

--- a/solution.py
+++ b/solution.py
@@ -24,7 +24,8 @@
 AX, AY, AZ, AM = 0, 3, 4, 32
 BZ, BY, BX, BM = 40, 47, 48, 72
 N_W = 76
-VIA = (2, 3)
+VIA = (3,)
+EARLY = 1
 
 
 def kernel(so_ref, lens_ref, q_hbm, k_ref, v_ref, w_ref, out_ref,
@@ -165,11 +166,17 @@
             own_mate(g).start()
 
     def kv_via(g):
+        if g not in VIA:
+            return
+
         @pl.when(x == 3)
         def _():
             own_via(g).start()
 
     def kv_on(g):
+        if g not in VIA:
+            return
+
         @pl.when(x == 0)
         def _():
             own_via(g).wait_recv()
@@ -325,51 +332,86 @@
         go(*az((1,), 0), am[0])
 
     def at2():
-        kv_on(2)
         got(*bz(3))
         go(*bx((7,), 1), bm[0])
+        kv_on(2)
 
     def at3():
-        kv_late(1)
         got(*az((2, 3), 0))
         go(*az((2, 3), 1))
+        kv_late(1)
 
     def at4():
-        kv_pass(2)
         got(*az((1,), 0))
         go(*az((1,), 1), am[1], am[2])
+        got(*bx((0, 1, 2, 3), 1))
+        go(*bx((0, 1, 2, 3), 2))
+        kv_pass(2)
+        go(*bx((0, 1), 0))
 
     def at5():
         kv_on(3)
-        got(*bx((0, 1, 2, 3), 1))
-        go(*bx((0, 1, 2, 3), 2))
 
     def at6():
         got(*az((0, 2), 1))
         go(*az((0, 2), 2))
 
     def at7():
-        kv_late(2)
         got(*az((3, 1), 1))
         go(*az((3, 1), 2), am[3], am[4])
+        got(*bx((4, 5, 6, 7), 1))
+        go(*bx((4, 5, 6, 7), 2), bm[2])
+        kv_late(2)
 
     def at8():
         kv_pass(3)
-        got(*bx((4, 5, 6, 7), 1))
-        go(*bx((4, 5, 6, 7), 2), bm[2])
-        go(*bx((0, 1, 2, 3), 0))
+        go(*bx((2, 3, 4, 5, 6, 7), 0))
 
     def at9():
         got(*az((0, 2), 2))
         go(*az((0, 2), 3))
-        go(*bx((4, 5, 6, 7), 0))
 
     def at11():
-        kv_late(3)
         got(*az((3, 1), 2))
         go(*az((3, 1), 3), am[5], am[6])
+        kv_late(3)
 
     before = {1: at1, 2: at2, 3: at3, 4: at4, 5: at5, 6: at6, 7: at7, 8: at8, 9: at9, 11: at11}
+
+    def both_parts(g):
+        def part(at):
+            a = att[at]
+            acca[...] += jnp.dot(a, wa[at].reshape(ROWS, NA), preferred_element_type=F32)
+            accb[...] += jnp.dot(a, wb[at].reshape(ROWS, NB), preferred_element_type=F32)
+
+        def side(k, carry):
+            head = lax.rem(h + k, 2)
+
+            @pl.when(k == 1)
+            def _():
+                for b in range(4):
+                    att_copy(1 - h, g, b).wait_recv()
+
+            part(4 * head + g)
+            return carry
+
+        lax.fori_loop(0, 2, side, 0)
+
+    def project_early():
+        got(*az((0, 1, 2, 3), 3))
+        go(am[7])
+        got(*bx(range(8), 2))
+        go(bm[3])
+        got(*bx(range(8), 0))
+        go(bm[1])
+        got(*am)
+        got(*bm)
+
+        def each(g, carry):
+            both_parts(g)
+            return carry
+
+        lax.fori_loop(0, 3, each, 0)
 
     lane = lax.broadcasted_iota(jnp.int32, (BLK, WIN), 1).astype(F32)
     row = lax.broadcasted_iota(jnp.int32, (BLK, BLK), 0)
@@ -377,16 +419,21 @@
 
     def unit(i, carry):
         g, b = lax.div(i, 4), lax.rem(i, 4)
+        @pl.when(i > 0)
+        def _():
+            att_copy(h, lax.div(i - 1, 4), lax.rem(i - 1, 4)).start()
+
         for at, run in before.items():
             pl.when(i == at)(run)
 
+        @pl.when((i == 12) & (x < EARLY))
+        def _():
+            project_early()
+
+
         @pl.when(b == 0)
         def _():
             kv_rest(g)
-
-        @pl.when(i > 0)
-        def _():
-            att_copy(h, lax.div(i - 1, 4), lax.rem(i - 1, 4)).start()
 
         q4 = held(q_ref, b, pl.ds(pl.multiple_of(g * 4 * HD, 4 * HD), 4 * HD))
         q = jnp.concatenate([q4[:, j * HD:(j + 1) * HD] for j in range(4)], axis=0)
@@ -413,40 +460,46 @@
     lax.fori_loop(0, 16, unit, 0)
     att_copy(h, 3, 3).start()
 
-    def project_a(j, carry):
-        d = lax.rem(lax.div(j + 1, 2) * (2 * lax.rem(j, 2) - 1) + 8, 8)
-        at = lax.rem(z + 8 - d, 8)
-
-        @pl.when(j == 7)
-        def _():
-            got(*az((0, 1, 2, 3), 3))
-            go(am[7])
-
-        for i in range(8):
-            @pl.when(j == i)
-            def _(i=i):
-                got(am[i])
-
-        @pl.when(lax.div(at, 4) == 1 - h)
-        def _():
-            for b in range(4):
-                att_copy(1 - h, lax.rem(at, 4), b).wait_recv()
-
-        acca[...] += jnp.dot(att[at], wa[at].reshape(ROWS, NA), preferred_element_type=F32)
-        return carry
-
-    lax.fori_loop(0, 8, project_a, 0)
-    got(*bx(range(8), 2))
-    go(bm[3])
-    got(*bx(range(8), 0))
-    go(bm[1])
-    got(*bm)
-
-    def project_b(at, carry):
-        accb[...] += jnp.dot(att[at], wb[at].reshape(ROWS, NB), preferred_element_type=F32)
-        return carry
-
-    lax.fori_loop(0, 8, project_b, 0)
+    @pl.when(x < EARLY)
+    def _():
+        both_parts(3)
+
+    @pl.when(x >= EARLY)
+    def _():
+        def project_a(j, carry):
+            d = lax.rem(lax.div(j + 1, 2) * (2 * lax.rem(j, 2) - 1) + 8, 8)
+            at = lax.rem(z + 8 - d, 8)
+
+            @pl.when(j == 7)
+            def _():
+                got(*az((0, 1, 2, 3), 3))
+                go(am[7])
+
+            for i in range(8):
+                @pl.when(j == i)
+                def _(i=i):
+                    got(am[i])
+
+            @pl.when(lax.div(at, 4) == 1 - h)
+            def _():
+                for b in range(4):
+                    att_copy(1 - h, lax.rem(at, 4), b).wait_recv()
+
+            acca[...] += jnp.dot(att[at], wa[at].reshape(ROWS, NA), preferred_element_type=F32)
+            return carry
+
+        lax.fori_loop(0, 8, project_a, 0)
+        got(*bx(range(8), 2))
+        go(bm[3])
+        got(*bx(range(8), 0))
+        go(bm[1])
+        got(*bm)
+
+        def project_b(at, carry):
+            accb[...] += jnp.dot(att[at], wb[at].reshape(ROWS, NB), preferred_element_type=F32)
+            return carry
+
+        lax.fori_loop(0, 8, project_b, 0)
 
     def placed(ref, j):
         part = ref[3 * BLK:4 * BLK, :]
@@ -476,13 +529,13 @@
     vmem = pl.BlockSpec(memory_space=pltpu.VMEM)
     return pl.pallas_call(
         kernel,
-        out_shape=jax.ShapeDtypeStruct((ROWS, 2048), BF16),
+        out_shape=pltpu.VMEM((ROWS, 2048), BF16),
         in_specs=[pl.BlockSpec(memory_space=pltpu.SMEM), vmem, pl.BlockSpec(memory_space=pl.ANY), vmem, vmem, vmem],
         out_specs=vmem,
         scratch_shapes=[
             pltpu.VMEM((ROWS, 2048), BF16),
             pltpu.VMEM((NG, 18 * BLK, 2 * HD), BF16),
-            pltpu.VMEM((len(VIA), 4 * BLK, 2 * HD), BF16),
+            pltpu.VMEM((max(1, len(VIA)), 4 * BLK, 2 * HD), BF16),
             pltpu.VMEM((NZ, NY, NX, 2, 32, NA), BF16),
             pltpu.VMEM((NZ, NY, NX, 2, 32, NB), BF16),
             pltpu.VMEM((8, ROWS, 4 * HD), BF16),
@@ -491,8 +544,8 @@
             pltpu.VMEM((ROWS, 128), F32),
             pltpu.SemaphoreType.DMA((NG, 5)),
             pltpu.SemaphoreType.DMA((NG, 4)),
-            pltpu.SemaphoreType.DMA((len(VIA),)),
-            pltpu.SemaphoreType.DMA((len(VIA),)),
+            pltpu.SemaphoreType.DMA((max(1, len(VIA)),)),
+            pltpu.SemaphoreType.DMA((max(1, len(VIA)),)),
             pltpu.SemaphoreType.DMA((N_W,)),
             pltpu.SemaphoreType.DMA((N_W,)),
             pltpu.SemaphoreType.DMA((NG, 4)),
@@ -500,7 +553,7 @@
             pltpu.SemaphoreType.DMA,
         ],
         compiler_params=pltpu.CompilerParams(
-            collective_id=0, has_side_effects=True, vmem_limit_bytes=63 * 1024 * 1024),
+            collective_id=0, has_side_effects=True, vmem_limit_bytes=58 * 1024 * 1024),
         name="attend_project",
     )(span_order.T, doc_lengths.reshape(1, 128), queries, key_states, value_rows_stored, w_out)
 

time: 137 us -> 128 us (0.934)
  Pallas kernels: 133 us -> 125 us
  local copies, waits for them, and re-layouts: 3.16 us -> 1.32 us
    pallas_call x1, Pallas kernels: 133 us -> 125 us  [per_device(): pl.pallas_call(kernel, out_shape=pltpu.VMEM((ROWS, 2048), BF16), in_specs...]
    unnamed x1, local copies, waits for them, and re-layouts: 3.16 us -> 1.32 us
where the time goes in v2:
time: 128 us; the launch traced here: 126 us
  Pallas kernels  125 us (98%)
  local copies, waits for them, and re-layouts  1.32 us (1%)
    pallas_call x1, Pallas kernels, per_device(): pl.pallas_call(kernel, out_shape=pltpu.VMEM((ROWS, 2048), BF16), in_specs...  125 us

profile of v2, /device:TPU:8, one launch (start us, length us, event | category | flops | bytes accessed | tf_op | source)
XLA Modules:
  0.0 126.5 jit_solution(13454545628510995721)
XLA Ops:
  0.0 125.1 %attend_project.1 = bf16[512,2048]{1,0:T(8,128)(2,1)S(1)} custom-call(s32[4,128]{1,0:T(4,128)} %bitcast.2, s32[1,128]{1,0:T(1,128)} %bitcast.3, bf16[512,2048]{1,0:T(8,128)(2,1)} %q_hbm.1, bf16[512,512]{1,0:T(8,128)(2,1)} %k_ref.1, bf16[512,512]{1,0:T(8,128)(2,1)} %v_ref.1, bf16[32,2048]{1,0:T(8,128)(2,1)} %w_ref.1), custom_call_target="tpu_custom_call" | custom-call | tf_op jit(solution)/shard_map/attend_project/pallas_call | solution.py:530
  125.1 1.3 %copy.8 = bf16[512,2048]{1,0:T(8,128)(2,1)} copy(bf16[512,2048]{1,0:T(8,128)(2,1)S(1)} %attend_project.1) | data formatting | bytes 4194304

commit v3 on v2

--- a/solution.py
+++ b/solution.py
@@ -309,13 +309,13 @@
     go(ax[0])
     kv_send(2)
     kv_via(2)
+    kv_via(3)
     got(ax[1])
     go(ax[2], *az((2,), 0))
     got(*bz(0))
     go(*bz(1), *bx((1, 2), 1))
     kv_pass(1)
     kv_send(3)
-    kv_via(3)
     got(*bz(1))
     go(*bz(2), *bx((3, 4), 1))
     got(ax[2])
@@ -332,29 +332,38 @@
         go(*az((1,), 0), am[0])
 
     def at2():
+        kv_on(2)
+        kv_on(3)
         got(*bz(3))
         go(*bx((7,), 1), bm[0])
-        kv_on(2)
 
     def at3():
         got(*az((2, 3), 0))
         go(*az((2, 3), 1))
         kv_late(1)
+
+        @pl.when(x > 0)
+        def _():
+            kv_pass(2)
 
     def at4():
         got(*az((1,), 0))
         go(*az((1,), 1), am[1], am[2])
         got(*bx((0, 1, 2, 3), 1))
         go(*bx((0, 1, 2, 3), 2))
-        kv_pass(2)
+        @pl.when(x == 0)
+        def _():
+            kv_pass(2)
+
         go(*bx((0, 1), 0))
-
-    def at5():
-        kv_on(3)
 
     def at6():
         got(*az((0, 2), 1))
         go(*az((0, 2), 2))
+
+        @pl.when(x > 0)
+        def _():
+            kv_pass(3)
 
     def at7():
         got(*az((3, 1), 1))
@@ -364,7 +373,10 @@
         kv_late(2)
 
     def at8():
-        kv_pass(3)
+        @pl.when(x == 0)
+        def _():
+            kv_pass(3)
+
         go(*bx((2, 3, 4, 5, 6, 7), 0))
 
     def at9():
@@ -376,7 +388,7 @@
         go(*az((3, 1), 3), am[5], am[6])
         kv_late(3)
 
-    before = {1: at1, 2: at2, 3: at3, 4: at4, 5: at5, 6: at6, 7: at7, 8: at8, 9: at9, 11: at11}
+    before = {1: at1, 2: at2, 3: at3, 4: at4, 6: at6, 7: at7, 8: at8, 9: at9, 11: at11}
 
     def both_parts(g):
         def part(at):

time: 128 us -> 126 us (0.984)
  no operation moved by 1% of the time
where the time goes in v3:
time: 126 us; the launch traced here: 125 us
  Pallas kernels  124 us (98%)
  local copies, waits for them, and re-layouts  1.32 us (1%)
    pallas_call x1, Pallas kernels, per_device(): pl.pallas_call(kernel, out_shape=pltpu.VMEM((ROWS, 2048), BF16), in_specs...  124 us

profile of v3, /device:TPU:8, one launch (start us, length us, event | category | flops | bytes accessed | tf_op | source)
XLA Modules:
  0.0 125.5 jit_solution(9204533333725058038)
XLA Ops:
  0.0 124.1 %attend_project.1 = bf16[512,2048]{1,0:T(8,128)(2,1)S(1)} custom-call(s32[4,128]{1,0:T(4,128)} %bitcast.2, s32[1,128]{1,0:T(1,128)} %bitcast.3, bf16[512,2048]{1,0:T(8,128)(2,1)} %q_hbm.1, bf16[512,512]{1,0:T(8,128)(2,1)} %k_ref.1, bf16[512,512]{1,0:T(8,128)(2,1)} %v_ref.1, bf16[32,2048]{1,0:T(8,128)(2,1)} %w_ref.1), custom_call_target="tpu_custom_call" | custom-call | tf_op jit(solution)/shard_map/attend_project/pallas_call | solution.py:542
  124.1 1.3 %copy.8 = bf16[512,2048]{1,0:T(8,128)(2,1)} copy(bf16[512,2048]{1,0:T(8,128)(2,1)S(1)} %attend_project.1) | data formatting | bytes 4194304

commit v4 on v3

--- a/solution.py
+++ b/solution.py
@@ -342,19 +342,13 @@
         go(*az((2, 3), 1))
         kv_late(1)
 
-        @pl.when(x > 0)
-        def _():
-            kv_pass(2)
+        kv_pass(2)
 
     def at4():
         got(*az((1,), 0))
         go(*az((1,), 1), am[1], am[2])
         got(*bx((0, 1, 2, 3), 1))
         go(*bx((0, 1, 2, 3), 2))
-        @pl.when(x == 0)
-        def _():
-            kv_pass(2)
-
         go(*bx((0, 1), 0))
 
     def at6():
@@ -372,11 +366,11 @@
         go(*bx((4, 5, 6, 7), 2), bm[2])
         kv_late(2)
 
+        @pl.when(x == 0)
+        def _():
+            kv_pass(3)
+
     def at8():
-        @pl.when(x == 0)
-        def _():
-            kv_pass(3)
-
         go(*bx((2, 3, 4, 5, 6, 7), 0))
 
     def at9():

time: 126 us -> 126 us (level)
  no operation moved by 1% of the time
where the time goes in v4:
time: 126 us; the launch traced here: 125 us
  Pallas kernels  124 us (98%)
  local copies, waits for them, and re-layouts  1.32 us (1%)
    pallas_call x1, Pallas kernels, per_device(): pl.pallas_call(kernel, out_shape=pltpu.VMEM((ROWS, 2048), BF16), in_specs...  124 us

profile of v4, /device:TPU:8, one launch (start us, length us, event | category | flops | bytes accessed | tf_op | source)
XLA Modules:
  0.0 125.5 jit_solution(7479536460960583300)
XLA Ops:
  0.0 124.1 %attend_project.1 = bf16[512,2048]{1,0:T(8,128)(2,1)S(1)} custom-call(s32[4,128]{1,0:T(4,128)} %bitcast.2, s32[1,128]{1,0:T(1,128)} %bitcast.3, bf16[512,2048]{1,0:T(8,128)(2,1)} %q_hbm.1, bf16[512,512]{1,0:T(8,128)(2,1)} %k_ref.1, bf16[512,512]{1,0:T(8,128)(2,1)} %v_ref.1, bf16[32,2048]{1,0:T(8,128)(2,1)} %w_ref.1), custom_call_target="tpu_custom_call" | custom-call | tf_op jit(solution)/shard_map/attend_project/pallas_call | solution.py:536
  124.1 1.3 %copy.8 = bf16[512,2048]{1,0:T(8,128)(2,1)} copy(bf16[512,2048]{1,0:T(8,128)(2,1)S(1)} %attend_project.1) | data formatting | bytes 4194304
